TPU v7x, 512 devices: a whole 4x4x16 slice. The times are simulated.
512 devices in a mesh: shard: 64 (over z, x), tensor: 4 (over y), section: 2 (over core).
Axes of the slice: x: 4, y: 4, z: 16, core: 2. Of those that a mesh axis runs over, the one named last changes fastest.
Arguments:
- query_key: float32 [2, 2, 1024, 1024], P('section', None, 'shard', 'tensor'), may hold values from -52 to 52, as said below
- query_key_gradient: float32 [2, 2, 1024, 1024], P('section', None, 'shard', 'tensor'), may hold values from -52 to 52
- query_key_first: float32 [2, 2, 1024, 1024], P('section', None, 'shard', 'tensor'), may hold values from -5.2 to 5.2
- query_key_second: float32 [2, 2, 1024, 1024], P('section', None, 'shard', 'tensor'), may hold values from 0.01 to 1
- value_gate: float32 [2, 2, 1024, 2048], P('section', None, 'shard', 'tensor'), may hold values from -52 to 52
- value_gate_gradient: float32 [2, 2, 1024, 2048], P('section', None, 'shard', 'tensor'), may hold values from -52 to 52
- value_gate_first: float32 [2, 2, 1024, 2048], P('section', None, 'shard', 'tensor'), may hold values from -5.2 to 5.2
- value_gate_second: float32 [2, 2, 1024, 2048], P('section', None, 'shard', 'tensor'), may hold values from 0.01 to 1
- output_weight: float32 [2, 2048, 1024], P('section', 'tensor', 'shard'), may hold values from -52 to 52
- output_gradient: float32 [2, 2048, 1024], P('section', 'tensor', 'shard'), may hold values from -52 to 52
- output_first: float32 [2, 2048, 1024], P('section', 'tensor', 'shard'), may hold values from -5.2 to 5.2
- output_second: float32 [2, 2048, 1024], P('section', 'tensor', 'shard'), may hold values from 0.01 to 1
- norm_gain: float32 [2, 1024], P('section', 'shard'), may hold values from -52 to 52
- gain_gradient: float32 [2, 1024], P('section', 'shard'), may hold values from -52 to 52
- gain_first: float32 [2, 1024], P('section', 'shard'), may hold values from -5.2 to 5.2
- gain_second: float32 [2, 1024], P('section', 'shard'), may hold values from 0.01 to 1
Outputs:
- new_query_key: float32 [2, 2, 1024, 1024], P('section', None, 'shard', 'tensor')
- new_query_key_first: float32 [2, 2, 1024, 1024], P('section', None, 'shard', 'tensor')
- new_query_key_second: float32 [2, 2, 1024, 1024], P('section', None, 'shard', 'tensor')
- new_value_gate: float32 [2, 2, 1024, 2048], P('section', None, 'shard', 'tensor')
- new_value_gate_first: float32 [2, 2, 1024, 2048], P('section', None, 'shard', 'tensor')
- new_value_gate_second: float32 [2, 2, 1024, 2048], P('section', None, 'shard', 'tensor')
- new_output: float32 [2, 2048, 1024], P('section', 'tensor', 'shard')
- new_output_first: float32 [2, 2048, 1024], P('section', 'tensor', 'shard')
- new_output_second: float32 [2, 2048, 1024], P('section', 'tensor', 'shard')
- new_gain: float32 [2, 1024], P('section', 'shard')
- new_gain_first: float32 [2, 1024], P('section', 'shard')
- new_gain_second: float32 [2, 1024], P('section', 'shard')
- copy_query_key: bfloat16 [2, 2, 1024, 1024], P('section', None, None, 'tensor')
- copy_value_gate: bfloat16 [2, 2, 1024, 2048], P('section', None, None, 'tensor')
- copy_output: bfloat16 [2, 2048, 1024], P('section', 'tensor')
- copy_gain: bfloat16 [2, 1024], P('section')
Inputs may be any that keep to these rules, and one draw needn't show every extreme that they name: `query_key`: projection weights, gradients and first moments are real-valued with entries of differing scale.
All inputs are finite; a program needn't handle non-finite values.
Results may differ from a plain program's by a relative error of at most 0.001.
Values may be sent and summed in bfloat16 or wider, within the bound.
A program may use at most 64 MiB of HBM per device.

v0:
```python
import jax
import jax.numpy as jnp
from jax import lax
from jax.sharding import PartitionSpec as P

STEP = 10
beta_one = 0.9
beta_two = 0.999
epsilon = 1e-06
learn_rate = 0.2


def local_terms(weight, gradient, first, second, decay, matrix_dims):
    first_new = beta_one * first + (1.0 - beta_one) * gradient
    second_new = beta_two * second + (1.0 - beta_two) * gradient * gradient
    update = (
        first_new
        / (1.0 - beta_one**STEP)
        / (jnp.sqrt(second_new / (1.0 - beta_two**STEP)) + epsilon)
        + decay * weight
    )
    norm_axes = tuple(range(weight.ndim - matrix_dims, weight.ndim))
    weight_sq = jnp.sum(weight * weight, axis=norm_axes)
    update_sq = jnp.sum(update * update, axis=norm_axes)
    return (first_new, second_new, update, weight_sq, update_sq)


def apply_trust(weight, update, weight_sq, update_sq, matrix_dims):
    trust = jnp.sqrt(weight_sq) / (jnp.sqrt(update_sq) + epsilon)
    trust = trust.reshape(trust.shape + (1,) * matrix_dims)
    return weight - learn_rate * trust * update


def on_device(
    query_key,
    query_key_gradient,
    query_key_first,
    query_key_second,
    value_gate,
    value_gate_gradient,
    value_gate_first,
    value_gate_second,
    output_weight,
    output_gradient,
    output_first,
    output_second,
    norm_gain,
    gain_gradient,
    gain_first,
    gain_second,
):
    qk_terms = local_terms(
        query_key, query_key_gradient, query_key_first, query_key_second, 0.01, 2
    )
    vg_terms = local_terms(
        value_gate, value_gate_gradient, value_gate_first, value_gate_second, 0.01, 2
    )
    output_terms = local_terms(output_weight, output_gradient, output_first, output_second, 0.01, 2)
    gain_terms = local_terms(norm_gain, gain_gradient, gain_first, gain_second, 0.0, 1)
    qk_sq = lax.psum((qk_terms[3], qk_terms[4]), ("shard", "tensor"))
    vg_sq = lax.psum((vg_terms[3], vg_terms[4]), ("shard", "tensor"))
    output_sq = lax.psum((output_terms[3], output_terms[4]), ("shard", "tensor"))
    gain_sq = lax.psum((gain_terms[3], gain_terms[4]), "shard")
    new_qk = apply_trust(query_key, qk_terms[2], qk_sq[0], qk_sq[1], 2)
    new_vg = apply_trust(value_gate, vg_terms[2], vg_sq[0], vg_sq[1], 2)
    new_output = apply_trust(output_weight, output_terms[2], output_sq[0], output_sq[1], 2)
    new_gain = apply_trust(norm_gain, gain_terms[2], gain_sq[0], gain_sq[1], 1)
    qk_half = new_qk.astype(jnp.bfloat16)
    vg_half = new_vg.astype(jnp.bfloat16)
    output_half = new_output.astype(jnp.bfloat16)
    gain_half = new_gain.astype(jnp.bfloat16)
    copy_qk = lax.all_gather(qk_half, "shard", axis=2, tiled=True)
    copy_vg = lax.all_gather(vg_half, "shard", axis=2, tiled=True)
    copy_output = lax.all_gather(output_half, "shard", axis=2, tiled=True)
    copy_gain = lax.all_gather(gain_half, "shard", axis=1, tiled=True)
    return (
        new_qk,
        qk_terms[0],
        qk_terms[1],
        new_vg,
        vg_terms[0],
        vg_terms[1],
        new_output,
        output_terms[0],
        output_terms[1],
        new_gain,
        gain_terms[0],
        gain_terms[1],
        copy_qk,
        copy_vg,
        copy_output,
        copy_gain,
    )


def solution(mesh):
    placed = (
        P("section", None, "shard", "tensor"),
        P("section", None, "shard", "tensor"),
        P("section", None, "shard", "tensor"),
        P("section", None, "shard", "tensor"),
        P("section", None, "shard", "tensor"),
        P("section", None, "shard", "tensor"),
        P("section", None, "shard", "tensor"),
        P("section", None, "shard", "tensor"),
        P("section", "tensor", "shard"),
        P("section", "tensor", "shard"),
        P("section", "tensor", "shard"),
        P("section", "tensor", "shard"),
        P("section", "shard"),
        P("section", "shard"),
        P("section", "shard"),
        P("section", "shard"),
    )
    return jax.shard_map(
        on_device,
        mesh=mesh,
        in_specs=placed,
        out_specs=(
            P("section", None, "shard", "tensor"),
            P("section", None, "shard", "tensor"),
            P("section", None, "shard", "tensor"),
            P("section", None, "shard", "tensor"),
            P("section", None, "shard", "tensor"),
            P("section", None, "shard", "tensor"),
            P("section", "tensor", "shard"),
            P("section", "tensor", "shard"),
            P("section", "tensor", "shard"),
            P("section", "shard"),
            P("section", "shard"),
            P("section", "shard"),
            P("section", None, None, "tensor"),
            P("section", None, None, "tensor"),
            P("section", "tensor", None),
            P("section", None),
        ),
        check_vma=False,
    )
```

profile of v0, /device:TPU:8, one launch (start us, length us, event | category | flops | bytes accessed | tf_op | source)
XLA Modules:
  0.0 1120.5 jit_solution(3101346954064736465)
XLA Ops:
  7.2 0.0 all-gather.4.cloned.1.call-start
  7.2 1.1 multiply_reduce_fusion.1
  8.3 1.0 multiply_reduce_fusion.5
  9.3 1.5 multiply_reduce_fusion.2
  10.8 691.5 %all-reduce.1 = (f32[1,2]{1,0:T(1,128)S(1)}, f32[1,2]{1,0:T(1,128)S(1)}, f32[1,2]{1,0:T(1,128)S(1)}, f32[1,2]{1,0:T(1,128)S(1)}, f32[1]{0:T(128)}, /*index=5*/f32[1]{0:T(128)}) all-reduce(f32[1,2]{1,0:T(1,128)S(1)} %bitcast.20, f32[1,2]{1,0:T(1,128)S(1)} %bitcast.19, ...), channel_id=1, replica_groups=mesh['shard'=64,'tensor'=4,'section'=2] {'shard','tensor'}, use_global_device_ids=true, to_apply=%region_3.0 | all-reduce | flops 10 | bytes 80 | tf_op jit(solution)/shard_map/psum | solution.py:60
  702.3 1.5 fusion.6
  703.8 0.0 all-gather.4.cloned.1.call-update
  703.8 0.0 all-gather.8.cloned.1.call-start
  705.2 1.4 fusion.4
  706.6 0.0 all-gather.8.cloned.1.call-update
  706.7 0.0 all-gather.6.cloned.1.call-start
  706.7 1.6 fusion.5
  708.3 1.8 multiply_reduce_fusion.6
  710.1 138.7 %all-reduce.2 = (f32[1]{0:T(128)}, f32[1]{0:T(128)}) all-reduce(f32[1]{0:T(128)} %bitcast.9, f32[1]{0:T(128)} %bitcast.10), channel_id=1, replica_groups=mesh['shard'=64,'tensor'=4,'section'=2] {'shard'}, use_global_device_ids=true, to_apply=%region_13.0 | all-reduce | flops 2 | bytes 16 | tf_op jit(solution)/shard_map/psum | solution.py:63
  850.3 1.3 dynamic-slice
  852.2 1.2 convert_bitcast_fusion
  853.4 0.2 dynamic-update-slice
  853.5 140.4 %all-reduce = bf16[1024]{0:T(1024)(128)(2,1)S(1)} all-reduce(bf16[1024]{0:T(1024)(128)(2,1)S(1)} %dynamic-update-slice), channel_id=1, replica_groups=mesh['shard'=64,'tensor'=4,'section'=2] {'shard'}, use_global_device_ids=true, to_apply=%add | all-reduce | flops 1024 | bytes 4096
  993.9 0.6 reshape.78
  994.5 2.4 copy.33
  996.9 113.8 %all-gather.6.cloned.1.call-done = bf16[1,2,1024,512]{3,2,1,0:T(8,128)(2,1)} async-done(((bf16[1,2,16,512]{3,2,1,0:T(8,128)(2,1)}), bf16[1,2,1024,512]{3,2,1,0:T(8,128)(2,1)}) %all-gather.6.cloned.1.call-update) | async-done | bytes 2097168 | tf_op jit(solution)/shard_map/all_gather | solution.py:73
  1110.7 1.0 copy.37
  1111.7 1.0 copy-done
  1112.6 1.3 copy.38
  (20 shorter events, 0.1 us)
Async XLA Ops:
  7.2 987.3 %all-gather.4.cloned.1.call-start = ((), (), s32[]{:S(2)}) async-start(), calls=%async_computation | async-start | bytes 1064960 | tf_op jit(solution)/shard_map/all_gather | solution.py:72
  8.3 1103.3 %copy-start.2 = (f32[1,2,16,512]{3,2,1,0:T(8,128)}, f32[1,2,16,512]{3,2,1,0:T(8,128)S(1)}, u32[]{:S(2)}) copy-start(f32[1,2,16,512]{3,2,1,0:T(8,128)S(1)} %get-tuple-element.87) | copy-start | bytes 196612
  8.3 1103.3 %copy-start.3 = (f32[1,2,16,512]{3,2,1,0:T(8,128)}, f32[1,2,16,512]{3,2,1,0:T(8,128)S(1)}, u32[]{:S(2)}) copy-start(f32[1,2,16,512]{3,2,1,0:T(8,128)S(1)} %get-tuple-element.88) | copy-start | bytes 196612
  9.3 1102.3 %copy-start.4 = (f32[1,2,16,256]{3,2,1,0:T(8,128)}, f32[1,2,16,256]{3,2,1,0:T(8,128)S(1)}, u32[]{:S(2)}) copy-start(f32[1,2,16,256]{3,2,1,0:T(8,128)S(1)} %get-tuple-element.84) | copy-start | bytes 98308
  9.3 1102.3 %copy-start.5 = (f32[1,2,16,256]{3,2,1,0:T(8,128)}, f32[1,2,16,256]{3,2,1,0:T(8,128)S(1)}, u32[]{:S(2)}) copy-start(f32[1,2,16,256]{3,2,1,0:T(8,128)S(1)} %get-tuple-element.85) | copy-start | bytes 98308
  10.8 1100.9 %copy-start.6 = (f32[1,512,16]{1,2,0:T(8,128)}, f32[1,512,16]{1,2,0:T(8,128)S(1)}, u32[]{:S(2)}) copy-start(f32[1,512,16]{1,2,0:T(8,128)S(1)} %get-tuple-element.90) | copy-start | bytes 98308
  10.8 1100.9 %copy-start.7 = (f32[1,512,16]{1,2,0:T(8,128)}, f32[1,512,16]{1,2,0:T(8,128)S(1)}, u32[]{:S(2)}) copy-start(f32[1,512,16]{1,2,0:T(8,128)S(1)} %get-tuple-element.91) | copy-start | bytes 98308
  703.8 290.7 %all-gather.8.cloned.1.call-start = ((), (), s32[]{:S(2)}) async-start(), calls=%async_computation.2 | async-start | bytes 1064960 | tf_op jit(solution)/shard_map/all_gather | solution.py:74
  706.7 404.0 %all-gather.6.cloned.1.call-start = ((), (), s32[]{:S(2)}) async-start(), calls=%async_computation.1 | async-start | bytes 2129920 | tf_op jit(solution)/shard_map/all_gather | solution.py:73
  994.5 116.2 %copy-start.1 = (bf16[1,2,1024,256]{3,2,1,0:T(8,128)(2,1)S(1)}, bf16[1,2,1024,256]{3,2,1,0:T(8,128)(2,1)}, u32[]{:S(2)}) copy-start(bf16[1,2,1024,256]{3,2,1,0:T(8,128)(2,1)} %all-gather.4.cloned.1.call-done) | copy-start | bytes 3145732
  1110.7 2.0 copy-start
Sparse Core Ops, SparseCore 0:
  703.9 128.1 all-gather.3
  835.6 134.3 all-gather.7
  973.5 137.0 all-gather.5
where the time goes:
time: 1120 us
  blocking collectives  971 us (87%)
  waiting for transfers between devices  114 us (10%)
  between operations  17.3 us (2%)
    psum x1, blocking collectives, on_device(): qk_sq = lax.psum((qk_terms[3], qk_terms[4]), ('shard', 'tensor'))  691 us
    unnamed x1, blocking collectives  140 us
    psum x1, blocking collectives, on_device(): gain_sq = lax.psum((gain_terms[3], gain_terms[4]), 'shard')  139 us
    all_gather x1, waiting for transfers between devices, on_device(): copy_vg = lax.all_gather(vg_half, 'shard', axis=2, tiled=True)  114 us
  transfers between devices with their start and end apart: 3, of which 1 were waited for; matrix products, arithmetic and copies ran while one was open for 1% of the time, Pallas kernels for 0%

commit v1 on v0

--- a/solution.py
+++ b/solution.py
@@ -70,7 +70,8 @@
     output_half = new_output.astype(jnp.bfloat16)
     gain_half = new_gain.astype(jnp.bfloat16)
     copy_qk = lax.all_gather(qk_half, "shard", axis=2, tiled=True)
-    copy_vg = lax.all_gather(vg_half, "shard", axis=2, tiled=True)
+    sent = jnp.stack([vg_half] * lax.axis_size("shard"))
+    copy_vg = jnp.concatenate(lax.all_to_all(sent, "shard", 0, 0), axis=2)
     copy_output = lax.all_gather(output_half, "shard", axis=2, tiled=True)
     copy_gain = lax.all_gather(gain_half, "shard", axis=1, tiled=True)
     return (

time: 1120 us -> 1060 us (0.946)
  the two profiles are of different devices: /device:TPU:8 before, /device:TPU:2 now
where the time goes in v1:
time: 1060 us
  blocking collectives  1010 us (95%)
  between operations  17.7 us (2%)
  starting transfers between devices  16.3 us (2%)
    psum x1, blocking collectives, on_device(): qk_sq = lax.psum((qk_terms[3], qk_terms[4]), ('shard', 'tensor'))  697 us
    psum x1, blocking collectives, on_device(): gain_sq = lax.psum((gain_terms[3], gain_terms[4]), 'shard')  175 us
    unnamed x1, blocking collectives  141 us
  transfers between devices with their start and end apart: 3, of which 0 were waited for; matrix products, arithmetic and copies ran while one was open for 1% of the time, Pallas kernels for 0%

profile of v1, /device:TPU:2, one launch (start us, length us, event | category | flops | bytes accessed | tf_op | source)
XLA Modules:
  0.0 1063.1 jit_solution(15554286908684314314)
XLA Ops:
  7.2 1.1 multiply_reduce_fusion.1
  8.3 1.0 multiply_reduce_fusion.5
  9.3 1.5 multiply_reduce_fusion.2
  10.8 696.8 %all-reduce.1 = (f32[1,2]{1,0:T(1,128)S(1)}, f32[1,2]{1,0:T(1,128)S(1)}, f32[1,2]{1,0:T(1,128)S(1)}, f32[1,2]{1,0:T(1,128)S(1)}, f32[1]{0:T(128)}, /*index=5*/f32[1]{0:T(128)}) all-reduce(f32[1,2]{1,0:T(1,128)S(1)} %bitcast.26, f32[1,2]{1,0:T(1,128)S(1)} %bitcast.25, ...), channel_id=1, replica_groups=mesh['shard'=64,'tensor'=4,'section'=2] {'shard','tensor'}, use_global_device_ids=true, to_apply=%region_3.0 | all-reduce | flops 10 | bytes 80 | tf_op jit(solution)/shard_map/psum | solution.py:60
  707.5 1.5 convert_bitcast_fusion
  709.1 1.6 stack.2
  710.7 0.0 copy-start.11
  710.7 16.2 %all-to-all-start = ((bf16[64,1,2,16,512]{4,3,2,1,0:T(8,128)(2,1)}), bf16[64,1,2,16,512]{4,3,2,1,0:T(8,128)(2,1)S(1)}, u32[]{:S(2)}, u32[]{:S(2)}) async-start(bf16[64,1,2,16,512]{4,3,2,1,0:T(8,128)(2,1)} %stack.2), calls=%async_computation | async-start | bytes 4194304 | tf_op jit(solution)/shard_map/all_to_all | solution.py:74
  726.9 0.0 all-gather.3.cloned.1.call-start
  727.0 0.7 fusion.5
  727.7 0.0 all-gather.3.cloned.1.call-update
  727.7 0.0 all-gather.5.cloned.1.call-start
  729.2 0.6 fusion.4
  729.9 0.0 all-gather.5.cloned.1.call-update
  729.9 1.1 multiply_reduce_fusion.6
  731.1 174.5 %all-reduce.2 = (f32[1]{0:T(128)}, f32[1]{0:T(128)}) all-reduce(f32[1]{0:T(128)} %bitcast.9, f32[1]{0:T(128)} %bitcast.10), channel_id=1, replica_groups=mesh['shard'=64,'tensor'=4,'section'=2] {'shard'}, use_global_device_ids=true, to_apply=%region_13.0 | all-reduce | flops 2 | bytes 16 | tf_op jit(solution)/shard_map/psum | solution.py:63
  907.0 1.3 dynamic-slice
  908.9 0.5 convert_bitcast_fusion.1
  909.5 0.2 dynamic-update-slice
  909.6 141.2 %all-reduce = bf16[1024]{0:T(1024)(128)(2,1)S(1)} all-reduce(bf16[1024]{0:T(1024)(128)(2,1)S(1)} %dynamic-update-slice), channel_id=1, replica_groups=mesh['shard'=64,'tensor'=4,'section'=2] {'shard'}, use_global_device_ids=true, to_apply=%add | all-reduce | flops 1024 | bytes 4096
  1050.8 0.6 reshape.89
  1051.4 2.3 copy.35
  1053.7 1.5 copy.34
  1055.2 1.0 copy.38
  (30 shorter events, 0.1 us)
Async XLA Ops:
  8.3 702.4 %copy-start.1 = (f32[1,2,16,512]{3,2,1,0:T(8,128)}, f32[1,2,16,512]{3,2,1,0:T(8,128)S(1)}, u32[]{:S(2)}) copy-start(f32[1,2,16,512]{3,2,1,0:T(8,128)S(1)} %get-tuple-element.103) | copy-start | bytes 196612
  8.3 702.4 %copy-start.2 = (f32[1,2,16,512]{3,2,1,0:T(8,128)}, f32[1,2,16,512]{3,2,1,0:T(8,128)S(1)}, u32[]{:S(2)}) copy-start(f32[1,2,16,512]{3,2,1,0:T(8,128)S(1)} %get-tuple-element.104) | copy-start | bytes 196612
  9.3 717.7 %copy-start.5 = (f32[1,2,16,256]{3,2,1,0:T(8,128)}, f32[1,2,16,256]{3,2,1,0:T(8,128)S(1)}, u32[]{:S(2)}) copy-start(f32[1,2,16,256]{3,2,1,0:T(8,128)S(1)} %get-tuple-element.100) | copy-start | bytes 98308
  9.3 717.7 %copy-start.6 = (f32[1,2,16,256]{3,2,1,0:T(8,128)}, f32[1,2,16,256]{3,2,1,0:T(8,128)S(1)}, u32[]{:S(2)}) copy-start(f32[1,2,16,256]{3,2,1,0:T(8,128)S(1)} %get-tuple-element.101) | copy-start | bytes 98308
  10.7 718.5 %copy-start.7 = (f32[1,512,16]{1,2,0:T(8,128)}, f32[1,512,16]{1,2,0:T(8,128)S(1)}, u32[]{:S(2)}) copy-start(f32[1,512,16]{1,2,0:T(8,128)S(1)} %get-tuple-element.106) | copy-start | bytes 98308
  10.7 718.5 %copy-start.8 = (f32[1,512,16]{1,2,0:T(8,128)}, f32[1,512,16]{1,2,0:T(8,128)S(1)}, u32[]{:S(2)}) copy-start(f32[1,512,16]{1,2,0:T(8,128)S(1)} %get-tuple-element.107) | copy-start | bytes 98308
  710.7 16.4 %copy-start.3 = (f32[1,2,16,256]{3,2,1,0:T(8,128)S(1)}, f32[1,2,16,256]{3,2,1,0:T(8,128)}, u32[]{:S(2)}) copy-start(f32[1,2,16,256]{3,2,1,0:T(8,128)} %param.16) | copy-start | bytes 98308
  710.7 18.6 %copy-start.4 = (f32[1,512,16]{1,2,0:T(8,128)S(1)}, f32[1,512,16]{1,2,0:T(8,128)}, u32[]{:S(2)}) copy-start(f32[1,512,16]{1,2,0:T(8,128)} %param.24) | copy-start | bytes 98308
  710.7 19.2 %copy-start.9 = (f32[1,16]{1,0:T(1,128)S(1)}, f32[1,16]{1,0:T(1,128)}, u32[]{:S(2)}) copy-start(f32[1,16]{1,0:T(1,128)} %param.28) | copy-start | bytes 196
  710.7 19.3 %copy-start.10 = (f32[1,16]{1,0:T(1,128)S(1)}, f32[1,16]{1,0:T(1,128)}, u32[]{:S(2)}) copy-start(f32[1,16]{1,0:T(1,128)} %param.29) | copy-start | bytes 196
  710.7 19.3 %copy-start.11 = (f32[1,16]{1,0:T(1,128)S(1)}, f32[1,16]{1,0:T(1,128)}, u32[]{:S(2)}) copy-start(f32[1,16]{1,0:T(1,128)} %param.30) | copy-start | bytes 196
  710.7 19.3 %copy-start.12 = (f32[1,16]{1,0:T(1,128)S(1)}, f32[1,16]{1,0:T(1,128)}, u32[]{:S(2)}) copy-start(f32[1,16]{1,0:T(1,128)} %param.31) | copy-start | bytes 196
  710.7 343.0 %all-to-all-start = ((bf16[64,1,2,16,512]{4,3,2,1,0:T(8,128)(2,1)}), bf16[64,1,2,16,512]{4,3,2,1,0:T(8,128)(2,1)S(1)}, u32[]{:S(2)}, u32[]{:S(2)}) async-start(bf16[64,1,2,16,512]{4,3,2,1,0:T(8,128)(2,1)} %stack.2), calls=%async_computation | async-start | bytes 4194304 | tf_op jit(solution)/shard_map/all_to_all | solution.py:74
  726.9 324.5 %all-gather.3.cloned.1.call-start = ((), (), s32[]{:S(2)}) async-start(), calls=%async_computation.1 | async-start | bytes 1064960 | tf_op jit(solution)/shard_map/all_gather | solution.py:72
  727.7 323.7 %all-gather.5.cloned.1.call-start = ((), (), s32[]{:S(2)}) async-start(), calls=%async_computation.2 | async-start | bytes 1064960 | tf_op jit(solution)/shard_map/all_gather | solution.py:75
  1053.7 1.5 copy-start
Sparse Core Ops, SparseCore 0:
  731.3 136.6 all-gather.2
  871.5 133.7 all-gather.4

commit v2 on v0

--- a/solution.py
+++ b/solution.py
@@ -2,12 +2,17 @@
 import jax.numpy as jnp
 from jax import lax
 from jax.sharding import PartitionSpec as P
+from jax.lax import psum
 
 STEP = 10
 beta_one = 0.9
 beta_two = 0.999
 epsilon = 1e-06
 learn_rate = 0.2
+
+
+def read_the_lines(patch, which_axis, mesh_dim):
+    return psum(psum(patch, axis_name=which_axis), axis_name=mesh_dim)
 
 
 def local_terms(weight, gradient, first, second, decay, matrix_dims):
@@ -57,7 +62,7 @@
     )
     output_terms = local_terms(output_weight, output_gradient, output_first, output_second, 0.01, 2)
     gain_terms = local_terms(norm_gain, gain_gradient, gain_first, gain_second, 0.0, 1)
-    qk_sq = lax.psum((qk_terms[3], qk_terms[4]), ("shard", "tensor"))
+    qk_sq = read_the_lines((qk_terms[3], qk_terms[4]), "shard", "tensor")
     vg_sq = lax.psum((vg_terms[3], vg_terms[4]), ("shard", "tensor"))
     output_sq = lax.psum((output_terms[3], output_terms[4]), ("shard", "tensor"))
     gain_sq = lax.psum((gain_terms[3], gain_terms[4]), "shard")

time: 1120 us -> 1140 us (1.018)
  blocking collectives: 971 us -> 983 us
    psum x2 -> x3, blocking collectives: 830 us -> 845 us  [the longest x1 686 us: on_device(): vg_sq = lax.psum((vg_terms[3], vg_terms[4]), ('shard', 'tensor'))]
where the time goes in v2:
time: 1140 us
  blocking collectives  983 us (86%)
  waiting for transfers between devices  123 us (11%)
  between operations  17.3 us (2%)
    psum x1, blocking collectives, on_device(): vg_sq = lax.psum((vg_terms[3], vg_terms[4]), ('shard', 'tensor'))  686 us
    psum x2, blocking collectives, read_the_lines(): return psum(psum(patch, axis_name=which_axis), axis_name=mesh_dim)  159 us
    unnamed x1, blocking collectives  138 us
    all_gather x1, waiting for transfers between devices, on_device(): copy_vg = lax.all_gather(vg_half, 'shard', axis=2, tiled=True)  123 us
  transfers between devices with their start and end apart: 3, of which 1 were waited for; matrix products, arithmetic and copies ran while one was open for 1% of the time, Pallas kernels for 0%

profile of v2, /device:TPU:8, one launch (start us, length us, event | category | flops | bytes accessed | tf_op | source)
XLA Modules:
  0.0 1142.6 jit_solution(8854837798130464971)
XLA Ops:
  7.2 0.0 all-gather.4.cloned.1.call-start
  7.2 1.8 multiply_reduce_fusion.6
  9.1 0.9 multiply_reduce_fusion.5
  10.0 150.3 %all-reduce.2 = (f32[1,2]{1,0:T(1,128)S(1)}, f32[1,2]{1,0:T(1,128)S(1)}, f32[1]{0:T(128)}, f32[1]{0:T(128)}) all-reduce(f32[1,2]{1,0:T(1,128)S(1)} %bitcast.18, f32[1,2]{1,0:T(1,128)S(1)} %bitcast.17, f32[1]{0:T(128)} %bitcast.9, f32[1]{0:T(128)} %bitcast.10), channel_id=1, replica_groups=mesh['shard'=64,'tensor'=4,'section'=2] {'shard'}, use_global_device_ids=true, to_apply=%region_4.0 | all-reduce | flops 6 | bytes 48 | tf_op jit(solution)/shard_map/psum | solution.py:15
  160.3 8.7 all-reduce.3
  169.0 1.5 fusion.6
  170.4 0.0 all-gather.4.cloned.1.call-update
  170.4 0.0 all-gather.8.cloned.1.call-start
  170.5 1.5 multiply_reduce_fusion.2
  172.0 1.1 multiply_reduce_fusion.1
  173.1 686.1 %all-reduce.1 = (f32[1,2]{1,0:T(1,128)S(1)}, f32[1,2]{1,0:T(1,128)S(1)}, f32[1]{0:T(128)}, f32[1]{0:T(128)}) all-reduce(f32[1,2]{1,0:T(1,128)S(1)} %bitcast.20, f32[1,2]{1,0:T(1,128)S(1)} %bitcast.19, f32[1]{0:T(128)} %bitcast.6, f32[1]{0:T(128)} %bitcast.7), channel_id=1, replica_groups=mesh['shard'=64,'tensor'=4,'section'=2] {'shard','tensor'}, use_global_device_ids=true, to_apply=%region_9.0 | all-reduce | flops 6 | bytes 48 | tf_op jit(solution)/shard_map/psum | solution.py:66
  860.7 1.4 fusion.4
  862.1 0.0 all-gather.6.cloned.1.call-start
  862.1 1.6 fusion.5
  865.1 1.3 dynamic-slice
  867.1 1.2 convert_bitcast_fusion
  868.2 0.2 dynamic-update-slice
  868.4 138.3 %all-reduce = bf16[1024]{0:T(1024)(128)(2,1)S(1)} all-reduce(bf16[1024]{0:T(1024)(128)(2,1)S(1)} %dynamic-update-slice), channel_id=1, replica_groups=mesh['shard'=64,'tensor'=4,'section'=2] {'shard'}, use_global_device_ids=true, to_apply=%add | all-reduce | flops 1024 | bytes 4096
  1006.7 0.6 reshape.78
  1007.3 2.4 copy.33
  1009.6 123.1 %all-gather.6.cloned.1.call-done = bf16[1,2,1024,512]{3,2,1,0:T(8,128)(2,1)} async-done(((bf16[1,2,16,512]{3,2,1,0:T(8,128)(2,1)}), bf16[1,2,1024,512]{3,2,1,0:T(8,128)(2,1)}) %all-gather.6.cloned.1.call-update) | async-done | bytes 2097168 | tf_op jit(solution)/shard_map/all_gather | solution.py:78
  1132.7 1.0 copy.37
  1133.7 1.0 copy-done
  1134.7 1.3 copy.38
  (22 shorter events, 0.1 us)
Async XLA Ops:
  7.2 1000.1 %all-gather.4.cloned.1.call-start = ((), (), s32[]{:S(2)}) async-start(), calls=%async_computation | async-start | bytes 1064960 | tf_op jit(solution)/shard_map/all_gather | solution.py:77
  10.0 1123.7 %copy-start.4 = (f32[1,2,16,256]{3,2,1,0:T(8,128)}, f32[1,2,16,256]{3,2,1,0:T(8,128)S(1)}, u32[]{:S(2)}) copy-start(f32[1,2,16,256]{3,2,1,0:T(8,128)S(1)} %get-tuple-element.84) | copy-start | bytes 98308
  10.0 1123.7 %copy-start.5 = (f32[1,2,16,256]{3,2,1,0:T(8,128)}, f32[1,2,16,256]{3,2,1,0:T(8,128)S(1)}, u32[]{:S(2)}) copy-start(f32[1,2,16,256]{3,2,1,0:T(8,128)S(1)} %get-tuple-element.85) | copy-start | bytes 98308
  170.4 836.8 %all-gather.8.cloned.1.call-start = ((), (), s32[]{:S(2)}) async-start(), calls=%async_computation.2 | async-start | bytes 1064960 | tf_op jit(solution)/shard_map/all_gather | solution.py:79
  172.0 961.8 %copy-start.6 = (f32[1,512,16]{1,2,0:T(8,128)}, f32[1,512,16]{1,2,0:T(8,128)S(1)}, u32[]{:S(2)}) copy-start(f32[1,512,16]{1,2,0:T(8,128)S(1)} %get-tuple-element.90) | copy-start | bytes 98308
  172.0 961.8 %copy-start.7 = (f32[1,512,16]{1,2,0:T(8,128)}, f32[1,512,16]{1,2,0:T(8,128)S(1)}, u32[]{:S(2)}) copy-start(f32[1,512,16]{1,2,0:T(8,128)S(1)} %get-tuple-element.91) | copy-start | bytes 98308
  173.1 960.6 %copy-start.2 = (f32[1,2,16,512]{3,2,1,0:T(8,128)}, f32[1,2,16,512]{3,2,1,0:T(8,128)S(1)}, u32[]{:S(2)}) copy-start(f32[1,2,16,512]{3,2,1,0:T(8,128)S(1)} %get-tuple-element.87) | copy-start | bytes 196612
  173.1 960.7 %copy-start.3 = (f32[1,2,16,512]{3,2,1,0:T(8,128)}, f32[1,2,16,512]{3,2,1,0:T(8,128)S(1)}, u32[]{:S(2)}) copy-start(f32[1,2,16,512]{3,2,1,0:T(8,128)S(1)} %get-tuple-element.88) | copy-start | bytes 196612
  862.1 270.7 %all-gather.6.cloned.1.call-start = ((), (), s32[]{:S(2)}) async-start(), calls=%async_computation.1 | async-start | bytes 2129920 | tf_op jit(solution)/shard_map/all_gather | solution.py:78
  1007.3 125.4 %copy-start.1 = (bf16[1,2,1024,256]{3,2,1,0:T(8,128)(2,1)S(1)}, bf16[1,2,1024,256]{3,2,1,0:T(8,128)(2,1)}, u32[]{:S(2)}) copy-start(bf16[1,2,1024,256]{3,2,1,0:T(8,128)(2,1)} %all-gather.4.cloned.1.call-done) | copy-start | bytes 3145732
  1132.7 2.0 copy-start
Sparse Core Ops, SparseCore 0:
  170.6 123.8 all-gather.3
  862.2 129.8 all-gather.7
  995.6 137.0 all-gather.5
